TPU v7x, 32 devices: a whole 2x2x4 slice. The times are simulated.
32 devices in a mesh: ctx: 8 (over z, y), grp: 4 (over x, core).
Axes of the slice: x: 2, y: 2, z: 4, core: 2. Of those that a mesh axis runs over, the one named last changes fastest.
Arguments:
- channels: bfloat16 [4096, 5120], P(('ctx', 'grp')), may hold values from -6 to 6
- gates: bfloat16 [4096, 5120], P(('ctx', 'grp')), may hold values from -6 to 6
- b_proj: bfloat16 [4096, 128], P(('ctx', 'grp')), may hold values from -6 to 6
- c_proj: bfloat16 [4096, 128], P(('ctx', 'grp')), may hold values from -0.5 to 0.5
- step_size: bfloat16 [4096, 80], P(('ctx', 'grp')), may hold values from 0.001 to 1, as said below
- log_decay: bfloat16 [4096, 80], P(('ctx', 'grp')), may hold values from -1 to 0, as said below
- skip_gain: float32 [80], P('grp'), may hold values from 0.5 to 2
- norm_gain: float32 [5120], P('grp'), may hold values from 0.1 to 1.9
- out_weight: bfloat16 [5120, 2560], P('grp'), may hold values from -0.078125 to 0.078125
Outputs:
- layer_out: bfloat16 [4096, 2560], P(('ctx', 'grp'))
Inputs may be any that keep to these rules, and one draw needn't show every extreme that they name: `step_size`: each token's step of each head is positive. `log_decay`: each token's log decay of each head is negative.
All inputs are finite; a program needn't handle non-finite values.
Results may differ from a plain program's by a relative error of at most 0.009.
Values may be sent and summed in bfloat16 or wider, within the bound.
A program may use at most 128 MiB of HBM per device.

v0:
```python
import jax
import jax.numpy as jnp
from jax import lax
from jax.sharding import PartitionSpec as P

HEADS = 80
HD = 64
NSTATE = 128
GROUP = 256


def prefix_2(value, axis, join, neutral):
    count, mine = (lax.axis_size(axis), lax.axis_index(axis))
    pieces = jax.tree.map(lambda part: lax.all_gather(part, axis), value)
    so_far = jax.tree.map(
        lambda part, zero: jnp.full_like(part, 0) + jnp.asarray(zero, part.dtype), value, neutral
    )

    def turn(position, so_far):
        longer = join(so_far, jax.tree.map(lambda part: part[position], pieces))
        return jax.tree.map(lambda new, old: jnp.where(position < mine, new, old), longer, so_far)

    return lax.fori_loop(0, count - 1, turn, so_far)


def local_scan(chan_heads, step_heads, decay_heads, b_rows, c_rows):
    highest = lax.Precision.HIGHEST
    piece_len = chan_heads.shape[0]
    nheads = step_heads.shape[1]
    blocks = piece_len // GROUP
    running = jnp.cumsum(decay_heads.astype(jnp.float32).reshape(blocks, GROUP, nheads), axis=1)
    running_t = jnp.transpose(running, (0, 2, 1))
    chan_f = chan_heads.astype(jnp.float32).reshape(piece_len, nheads, HD)
    inputs = (chan_f * step_heads.astype(jnp.float32)[:, :, None]).reshape(
        blocks, GROUP, nheads, HD
    )
    b_blocks = b_rows.reshape(blocks, GROUP, NSTATE)
    c_blocks = c_rows.reshape(blocks, GROUP, NSTATE)
    scores = jnp.einsum("qin,qjn->qij", c_blocks, b_blocks, preferred_element_type=jnp.float32)
    rows_at = lax.broadcasted_iota(jnp.int32, (GROUP, GROUP), 0)
    cols_at = lax.broadcasted_iota(jnp.int32, (GROUP, GROUP), 1)
    causal = rows_at >= cols_at
    spread = running_t[:, :, :, None] - running_t[:, :, None, :]
    weights = jnp.where(causal[None, None], jnp.exp(spread), 0.0) * scores[:, None]
    y_intra = jnp.einsum("qhij,qjhp->qihp", weights, inputs, precision=highest)
    tail_decay = jnp.exp(running[:, -1:, :] - running)
    b_float = b_blocks.astype(jnp.float32)
    c_float = c_blocks.astype(jnp.float32)
    group_states = jnp.einsum(
        "qjhp,qjn->qhpn", inputs * tail_decay[..., None], b_float, precision=highest
    )
    totals = jnp.exp(running[:, -1, :])

    def carry_step(carried, packed):
        factor, fresh_state = packed
        return (factor[:, None, None] * carried + fresh_state, carried)

    final_state, starts = lax.scan(
        carry_step, jnp.zeros((nheads, HD, NSTATE), jnp.float32), (totals, group_states)
    )
    y_inter = (
        jnp.einsum("qin,qhpn->qihp", c_float, starts, precision=highest)
        * jnp.exp(running)[..., None]
    )
    group_logs = running[:, -1, :]
    offsets = jnp.cumsum(group_logs, axis=0) - group_logs
    piece_cum = (running + offsets[:, None, :]).reshape(piece_len, nheads)
    piece_log = jnp.sum(group_logs, axis=0)
    local_out = (y_intra + y_inter).reshape(piece_len, nheads, HD)
    return (local_out, final_state, piece_log, piece_cum, chan_f)


def local(channels, gates, b_proj, c_proj, step_size, log_decay, skip_gain, norm_gain, out_weight):
    highest = lax.Precision.HIGHEST
    chan_heads, gate_heads, step_heads, decay_heads = (
        lax.all_to_all(channels, "grp", split_axis=1, concat_axis=0, tiled=True),
        lax.all_to_all(gates, "grp", split_axis=1, concat_axis=0, tiled=True),
        lax.all_to_all(step_size, "grp", split_axis=1, concat_axis=0, tiled=True),
        lax.all_to_all(log_decay, "grp", split_axis=1, concat_axis=0, tiled=True),
    )
    b_rows, c_rows = (
        lax.all_gather(b_proj, "grp", axis=0, tiled=True),
        lax.all_gather(c_proj, "grp", axis=0, tiled=True),
    )
    local_out, final_state, piece_log, piece_cum, chan_f = local_scan(
        chan_heads, step_heads, decay_heads, b_rows, c_rows
    )
    piece_factor = jnp.exp(piece_log)

    def combine(early_part, later_part):
        return (
            early_part[0] * later_part[0],
            later_part[0][:, None, None] * early_part[1] + later_part[1],
        )

    identity = (jnp.ones_like(piece_factor), jnp.zeros_like(final_state))
    prefix = prefix_2((piece_factor, final_state), "ctx", combine, identity)
    incoming = prefix[1]
    correction = jnp.einsum("tn,hpn->thp", c_rows.astype(jnp.float32), incoming, precision=highest)
    correction = correction * jnp.exp(piece_cum)[:, :, None]
    ssm_out = local_out + correction + skip_gain[None, :, None] * chan_f
    piece_len = chan_heads.shape[0]
    gated_out = ssm_out.reshape(piece_len, chan_heads.shape[1]) * jax.nn.silu(
        gate_heads.astype(jnp.float32)
    )
    row_squares = lax.psum(jnp.sum(gated_out * gated_out, axis=1), "grp")
    scale = lax.rsqrt(row_squares / (HEADS * HD) + 1e-05)
    normed = (gated_out * scale[:, None] * norm_gain[None, :]).astype(jnp.bfloat16)
    return lax.psum_scatter(
        jnp.dot(normed, out_weight, preferred_element_type=jnp.float32).astype(jnp.bfloat16),
        "grp",
        scatter_dimension=0,
        tiled=True,
    )


def solution(mesh):
    in_specs = (
        P(("ctx", "grp"), None),
        P(("ctx", "grp"), None),
        P(("ctx", "grp"), None),
        P(("ctx", "grp"), None),
        P(("ctx", "grp"), None),
        P(("ctx", "grp"), None),
        P("grp"),
        P("grp"),
        P("grp", None),
    )
    out_specs = P(("ctx", "grp"), None)
    return jax.shard_map(local, mesh=mesh, in_specs=in_specs, out_specs=out_specs, check_vma=False)
```

profile of v0, /device:TPU:0, one launch (start us, length us, event | category | flops | bytes accessed | tf_op | source)
XLA Modules:
  0.0 233.1 jit_solution(6459703165636211416)
XLA Ops:
  6.5 1.4 all_to_all.44
  7.9 4.2 %all-to-all-start.2 = ((bf16[128,4,20]{0,2,1:T(8,128)(2,1)}), bf16[128,4,20]{0,2,1:T(8,128)(2,1)S(1)}, u32[]{:S(2)}, u32[]{:S(2)}) async-start(bf16[128,4,20]{0,2,1:T(8,128)(2,1)} %all_to_all.44), calls=%async_computation.2 | async-start | bytes 49152 | tf_op jit(solution)/shard_map/all_to_all | solution.py:79
  12.1 5.8 %all_gather.17 = bf16[512,128]{1,0:T(8,128)(2,1)S(1)} all-gather(bf16[128,128]{1,0:T(8,128)(2,1)} %param.15), channel_id=1, replica_groups=mesh['ctx'=8,'grp'=4] {'grp'}, dimensions={0}, use_global_device_ids=true | all-gather | bytes 163840 | tf_op jit(solution)/shard_map/all_gather | solution.py:82
  17.9 2.4 %copy.51 = bf16[128,5120]{0,1:T(8,128)(2,1)} copy(bf16[128,5120]{1,0:T(8,128)(2,1)} %param.13) | data formatting | bytes 2621440 | tf_op args[0]
  20.9 3.3 %all-to-all-start.1 = ((bf16[128,4,20]{0,2,1:T(8,128)(2,1)}), bf16[128,4,20]{0,2,1:T(8,128)(2,1)S(1)}, u32[]{:S(2)}, u32[]{:S(2)}) async-start(bf16[128,4,20]{0,2,1:T(8,128)(2,1)} %all_to_all.42), calls=%async_computation.1 | async-start | bytes 49152 | tf_op jit(solution)/shard_map/all_to_all | solution.py:78
  24.3 1.2 reduce-window.6
  25.7 2.3 %all-to-all-done.1 = bf16[128,4,20]{0,2,1:T(8,128)(2,1)S(1)} async-done(((bf16[128,4,20]{0,2,1:T(8,128)(2,1)}), bf16[128,4,20]{0,2,1:T(8,128)(2,1)S(1)}, u32[]{:S(2)}, u32[]{:S(2)}) %all-to-all-start.1) | async-done | bytes 20512 | tf_op jit(solution)/shard_map/all_to_all | solution.py:78
  28.1 3.5 %all-to-all-start = ((bf16[128,4,1280]{0,2,1:T(8,128)(2,1)}), bf16[128,4,1280]{0,2,1:T(8,128)(2,1)S(1)}, u32[]{:S(2)}, u32[]{:S(2)}) async-start(bf16[128,4,1280]{0,2,1:T(8,128)(2,1)} %bitcast), calls=%async_computation | async-start | bytes 2621440 | tf_op jit(solution)/shard_map/all_to_all | solution.py:76
  33.5 15.3 %all-to-all-done = bf16[128,4,1280]{0,2,1:T(8,128)(2,1)S(1)} async-done(((bf16[128,4,1280]{0,2,1:T(8,128)(2,1)}), bf16[128,4,1280]{0,2,1:T(8,128)(2,1)S(1)}, u32[]{:S(2)}, u32[]{:S(2)}) %all-to-all-start) | async-done | bytes 1310752 | tf_op jit(solution)/shard_map/all_to_all | solution.py:76
  49.0 5.4 %copy.52 = f32[4,128,1280]{1,0,2:T(4,128)S(1)} copy(f32[4,128,1280]{1,2,0:T(8,128)S(1)} %convert_bitcast_fusion.1) | data formatting | bytes 5242880 | tf_op jit(solution)/shard_map/convert_element_type | solution.py:33
  54.5 3.3 %reshape.122 = f32[2,256,20,64]{1,0,3,2:T(2,128)} reshape(f32[4,128,1280]{1,0,2:T(4,128)S(1)} %copy.52) | data formatting | bytes 5242880 | tf_op jit(solution)/shard_map/convert_element_type | solution.py:33
  57.8 5.1 %broadcast_multiply_fusion = (f32[2,256,20,64]{1,0,3,2:T(2,128)S(1)}, f32[2,256,20,64]{1,0,3,2:T(2,128)}) fusion(f32[2,256,20]{1,0,2:T(2,128)S(1)} %get-tuple-element.189, f32[2,256,20,64]{1,0,3,2:T(2,128)} %reshape.122, f32[2,256,20]{1,0,2:T(2,128)S(1)} %reshape.123), kind=kLoop, calls=%fused_computation.39 | loop fusion | flops 1310720 | bytes 7946240 | tf_op jit(solution)/shard_map/mul | solution.py:50
  62.9 2.4 %fusion.22 = f32[2,20,64,128]{3,2,1,0:T(8,128)} fusion(bf16[2,256,128,1]{2,1,3,0:T(8,128)(2,1)S(1)} %bitcast.131, f32[2,256,20,64]{1,0,3,2:T(2,128)S(1)} %get-tuple-element.186), kind=kOutput, calls=%fused_computation.33 | convolution fusion | flops 1006632960 | bytes 4063232 | tf_op jit(solution)/shard_map/qjhp,qjn->qhpn/dot_general | solution.py:49
  65.3 4.3 %while.27 = (s32[]{:T(128)}, f32[20,64,128]{2,1,0:T(8,128)S(1)}, f32[2,20,64,128]{3,2,1,0:T(8,128)}, f32[2,20]{1,0:T(2,128)S(1)}, f32[2,20,64,128]{3,2,1,0:T(8,128)}, /*index=5*/s32[]{:T(128)}, s32[]{:T(128)}) while((s32[]{:T(128)}, f32[20,64,128]{2,1,0:T(8,128)S(1)}, f32[2,20,64,128]{3,2,1,0:T(8,128)}, f32[2,20]{1,0:T(2,128)S(1)}, ...), condition=%wide.region_3.4_spmd.clone, body=%wide.region_2.3_spmd.clone.sunk | while | flops 655363 | bytes 3277648 | solution.py:58
  65.3 0.9 bitcast_dynamic-update-slice_fusion.2
  66.2 1.2 bitcast_add_fusion.3
  67.5 0.9 bitcast_dynamic-update-slice_fusion.2
  68.4 1.2 bitcast_add_fusion.3
  69.6 0.8 copy-done
  70.5 2.5 %copy.68 = bf16[128,5120]{0,1:T(8,128)(2,1)} copy(bf16[128,5120]{1,0:T(8,128)(2,1)} %param.14) | data formatting | bytes 2621440 | tf_op args[1]
  72.9 4.3 %all-to-all-start.3 = ((bf16[128,4,1280]{0,2,1:T(8,128)(2,1)}), bf16[128,4,1280]{0,2,1:T(8,128)(2,1)}, u32[]{:S(2)}, u32[]{:S(2)}) async-start(bf16[128,4,1280]{0,2,1:T(8,128)(2,1)} %bitcast.127), calls=%async_computation.3 | async-start | bytes 2621440 | tf_op jit(solution)/shard_map/all_to_all | solution.py:77
  78.5 17.5 %all_gather.16 = bf16[512,128]{1,0:T(8,128)(2,1)S(1)} all-gather(bf16[128,128]{1,0:T(8,128)(2,1)} %param.16), channel_id=1, replica_groups=mesh['ctx'=8,'grp'=4] {'grp'}, dimensions={0}, use_global_device_ids=true | all-gather | bytes 163840 | tf_op jit(solution)/shard_map/all_gather | solution.py:83
  96.7 1.0 fusion.28
  97.7 1.4 copy.57
  100.0 22.7 %all-reduce = f32[160]{0:T(256)S(1)} all-reduce(f32[160]{0:T(256)S(1)} %exponential_dynamic-update-slice_fusion), channel_id=2, replica_groups=mesh['ctx'=8,'grp'=4] {'ctx'}, use_global_device_ids=true, to_apply=%add | all-reduce | flops 160 | bytes 1280
  124.2 2.1 reshape.125
  126.3 13.1 %fusion.2 = f32[2,20,64,256]{3,2,1,0:T(8,128)S(1)} fusion(f32[2,256,256]{2,1,0:T(8,128)} %fusion.28, f32[2,20,256]{2,1,0:T(8,128)} %copy.57, pred[256,256]{1,0:T(8,128)(4,1)S(1)} %copy-done.3, f32[2,256,20,64]{1,0,3,2:T(2,128)} %get-tuple-element.187), kind=kOutput, calls=%fused_computation.7 | convolution fusion | flops 2021130240 | bytes 5873664 | tf_op jit(solution)/shard_map/qhij,qjhp->qihp/dot_general | solution.py:45
  139.5 1.3 fusion.21
  140.9 1.9 copy.74
  142.7 1.6 copy.69
  144.3 1.7 convert_bitcast_fusion
  146.1 4.1 %copy.71 = f32[4,128,1280]{1,0,2:T(4,128)} copy(f32[4,128,1280]{2,1,0:T(8,128)} %convert_bitcast_fusion) | data formatting | bytes 5242880 | tf_op jit(solution)/shard_map/convert_element_type | solution.py:104
  150.2 4.1 %reshape.127 = f32[512,20,64]{0,2,1:T(8,128)} reshape(f32[4,128,1280]{1,0,2:T(4,128)} %copy.71) | data formatting | bytes 5242880 | tf_op jit(solution)/shard_map/convert_element_type | solution.py:104
  154.4 3.5 %all-gather.4.cloned.1.call-done = f32[160,64,128]{2,1,0:T(8,128)} async-done(((f32[20,64,128]{2,1,0:T(8,128)}), f32[160,64,128]{2,1,0:T(8,128)}) %all-gather.4.cloned.1.call-update) | async-done | bytes 5242896 | tf_op jit(solution)/shard_map/all_gather | solution.py:14
  157.9 8.9 %while.28 = (s32[]{:T(128)}, f32[20,64,128]{2,1,0:T(8,128)S(1)}, s32[]{:T(128)}, f32[8,20]{1,0:T(8,128)S(1)}, f32[8,20,64,128]{3,2,1,0:T(8,128)}, /*index=5*/s32[]{:T(128)}, s32[]{:T(128)}) while((s32[]{:T(128)}, f32[20,64,128]{2,1,0:T(8,128)S(1)}, s32[]{:T(128)}, f32[8,20]{1,0:T(8,128)S(1)}, f32[8,20,64,128]{3,2,1,0:T(8,128)}, ...), condition=%wide.region_6.7_spmd.clone, body=%wide.region_5.6_spmd.clone.sunk | while | flops 655364 | bytes 1966425 | solution.py:23
  157.9 1.2 fusion.40
  159.2 1.2 fusion.40
  160.5 1.2 fusion.40
  161.7 1.2 fusion.40
  163.0 1.2 fusion.40
  164.3 1.2 fusion.40
  165.6 1.2 fusion.40
  166.8 6.9 %multiply_reduce_fusion = (f32[512]{0:T(512)S(1)}, f32[512,20,64]{0,2,1:T(8,128)}) fusion(f32[512,20,64]{0,2,1:T(8,128)} %reshape.127, f32[512,20,64]{0,2,1:T(8,128)} %reshape.125, f32[20]{0:T(128)S(1)} %copy-done.7, f32[512,20,64]{0,2,1:T(8,128)} %bitcast.128, f32[512,20]{0,1:T(8,128)S(1)} %bitcast.139, f32[20,64,128]{2,1,0:T(8,128)S(1)} %get-tuple-element.129, ...), kind=kOutput, calls=%fused_computation.37 | convolution fusion | flops 1013841408 | bytes 11315280 | tf_op jit(solution)/shard_map/tn,hpn->thp/dot_general | solution.py:99
  173.7 3.2 %copy.70 = f32[512,1280]{1,0:T(8,128)} copy(f32[512,1280]{0,1:T(8,128)} %bitcast.129) | data formatting | bytes 5242880 | tf_op jit(solution)/shard_map/reshape | solution.py:103
  176.9 5.9 %psum.7 = f32[512]{0:T(512)S(1)} all-reduce(f32[512]{0:T(512)S(1)} %get-tuple-element.193), channel_id=1, replica_groups=mesh['ctx'=8,'grp'=4] {'grp'}, use_global_device_ids=true, to_apply=%region_9.10 | all-reduce | flops 512 | bytes 4096 | tf_op jit(solution)/shard_map/psum | solution.py:106
  182.9 2.6 %fusion.25 = bf16[512,1280]{1,0:T(8,128)(2,1)S(1)} fusion(f32[512,1280]{1,0:T(8,128)} %copy.70, bf16[128,4,1280]{2,0,1:T(8,128)(2,1)S(1)} %copy.69, f32[1280]{0:T(1024)S(1)} %copy-done.6, f32[512]{0:T(512)S(1)} %add_rsqrt_fusion), kind=kLoop, calls=%fused_computation.38 | loop fusion | flops 5898240 | bytes 5250048 | tf_op jit(solution)/shard_map/convert_element_type | solution.py:108
  185.5 7.7 %convolution_convert_fusion = bf16[512,2560]{1,0:T(8,128)(2,1)} fusion(bf16[512,1280]{1,0:T(8,128)(2,1)S(1)} %fusion.25, bf16[1280,2560]{1,0:T(8,128)(2,1)} %param.21), kind=kOutput, calls=%fused_computation.17 | convolution fusion | flops 3356753920 | bytes 10485760 | tf_op jit(solution)/shard_map/dot_general | solution.py:110
  193.2 33.1 %reduce-scatter.2.cloned.1.call-done = bf16[128,2560]{1,0:T(8,128)(2,1)} async-done(((bf16[512,2560]{1,0:T(8,128)(2,1)}), bf16[128,2560]{1,0:T(8,128)(2,1)}) %reduce-scatter.2.cloned.1.call-update) | async-done | bytes 655376 | tf_op jit(solution)/shard_map/reduce_scatter | solution.py:109
  (69 shorter events, 6.7 us)
Async XLA Ops:
  6.5 13.8 %copy-start.5 = (bf16[128,80]{0,1:T(8,128)(2,1)S(1)}, bf16[128,80]{0,1:T(8,128)(2,1)}, u32[]{:S(2)}) copy-start(bf16[128,80]{0,1:T(8,128)(2,1)} %param.17) | copy-start | bytes 61444
  7.9 13.0 %all-to-all-start.2 = ((bf16[128,4,20]{0,2,1:T(8,128)(2,1)}), bf16[128,4,20]{0,2,1:T(8,128)(2,1)S(1)}, u32[]{:S(2)}, u32[]{:S(2)}) async-start(bf16[128,4,20]{0,2,1:T(8,128)(2,1)} %all_to_all.44), calls=%async_computation.2 | async-start | bytes 49152 | tf_op jit(solution)/shard_map/all_to_all | solution.py:79
  20.9 7.1 %all-to-all-start.1 = ((bf16[128,4,20]{0,2,1:T(8,128)(2,1)}), bf16[128,4,20]{0,2,1:T(8,128)(2,1)S(1)}, u32[]{:S(2)}, u32[]{:S(2)}) async-start(bf16[128,4,20]{0,2,1:T(8,128)(2,1)} %all_to_all.42), calls=%async_computation.1 | async-start | bytes 49152 | tf_op jit(solution)/shard_map/all_to_all | solution.py:78
  28.1 20.8 %all-to-all-start = ((bf16[128,4,1280]{0,2,1:T(8,128)(2,1)}), bf16[128,4,1280]{0,2,1:T(8,128)(2,1)S(1)}, u32[]{:S(2)}, u32[]{:S(2)}) async-start(bf16[128,4,1280]{0,2,1:T(8,128)(2,1)} %bitcast), calls=%async_computation | async-start | bytes 2621440 | tf_op jit(solution)/shard_map/all_to_all | solution.py:76
  31.6 126.3 %all-gather.4.cloned.1.call-start = ((), (), s32[]{:S(2)}) async-start(), calls=%async_computation.6 | async-start | bytes 5898240 | tf_op jit(solution)/shard_map/all_gather | solution.py:14
  31.8 17.0 %copy-start.2 = (f32[2,20,256]{2,0,1:T(2,128)}, f32[2,20,256]{2,0,1:T(2,128)S(1)}, u32[]{:S(2)}) copy-start(f32[2,20,256]{2,0,1:T(2,128)S(1)} %reduce_window_sum.35) | copy-start | bytes 122884
  69.6 0.8 copy-start
  70.5 6.9 %copy-start.8 = (u32[32]{0:T(128)S(1)}, u32[32]{0:T(128)}, u32[]{:S(2)}) copy-start(u32[32]{0:T(128)} %constant.61) | copy-start | bytes 388
  72.9 69.8 %all-to-all-start.3 = ((bf16[128,4,1280]{0,2,1:T(8,128)(2,1)}), bf16[128,4,1280]{0,2,1:T(8,128)(2,1)}, u32[]{:S(2)}, u32[]{:S(2)}) async-start(bf16[128,4,1280]{0,2,1:T(8,128)(2,1)} %bitcast.127), calls=%async_computation.3 | async-start | bytes 2621440 | tf_op jit(solution)/shard_map/all_to_all | solution.py:77
  77.3 149.0 %reduce-scatter.2.cloned.1.call-start = ((), (), s32[]{:S(2)}) async-start(), calls=%async_computation.5 | async-start | bytes 3276800 | tf_op jit(solution)/shard_map/reduce_scatter | solution.py:109
  124.2 2.1 copy-start.3
  126.3 13.1 %copy-start.1 = (f32[2,20,64,128]{3,2,1,0:T(8,128)S(1)}, f32[2,20,64,128]{3,2,1,0:T(8,128)}, u32[]{:S(2)}) copy-start(f32[2,20,64,128]{3,2,1,0:T(8,128)} %get-tuple-element.127) | copy-start | bytes 3932164
  157.9 8.9 %copy-start.4 = (f32[3,8,2,256]{3,1,2,0:T(8,128)S(1)}, f32[3,8,2,256]{3,1,2,0:T(8,128)}, u32[]{:S(2)}) copy-start(f32[3,8,2,256]{3,1,2,0:T(8,128)} %copy.75) | copy-start | bytes 147460
  157.9 8.9 %copy-start.7 = (f32[20]{0:T(128)S(1)}, f32[20]{0:T(128)}, u32[]{:S(2)}) copy-start(f32[20]{0:T(128)} %param.19) | copy-start | bytes 244
  173.7 9.2 %copy-start.6 = (f32[1280]{0:T(1024)S(1)}, f32[1280]{0:T(1024)}, u32[]{:S(2)}) copy-start(f32[1280]{0:T(1024)} %param.20) | copy-start | bytes 15364
Sparse Core Ops, SparseCore 0:
  70.6 87.2 all-gather.3
  193.3 32.9 reduce-scatter.1
where the time goes:
time: 235 us; the launch traced here: 233 us
  waiting for transfers between devices  54.3 us (23%)
  blocking collectives  51.9 us (22%)
  local copies, waits for them, and re-layouts  38.9 us (17%)
  matrix products  32.5 us (14%)
  other arithmetic  25.6 us (11%)
  starting transfers between devices  15.4 us (7%)
  between operations  14.3 us (6%)
    reduce_scatter x1, waiting for transfers between devices, local(): lax.psum_scatter(jnp.dot(normed, out_weight, preferred_element_type=jnp.f...  33.1 us
    unnamed x1, blocking collectives  22.7 us
    all_gather x1, blocking collectives, local(): lax.all_gather(c_proj, 'grp', axis=0, tiled=True)  17.5 us
    all_to_all x1, waiting for transfers between devices, local(): lax.all_to_all(channels, 'grp', split_axis=1, concat_axis=0, tiled=True)  15.3 us
    dot_general x1, matrix products, local_scan(): y_intra = jnp.einsum('qhij,qjhp->qihp', weights, inputs, precision=highest)  13.1 us
    convert_element_type x3, local copies, waits for them, and re-layouts, local_scan(): chan_f = chan_heads.astype(jnp.float32).reshape(piece_len, nheads, HD)  10.9 us
    select_n x7, other arithmetic, turn(): jnp.where(position < mine, new, old)  8.64 us
    convert_element_type x2, local copies, waits for them, and re-layouts, local(): gate_heads.astype(jnp.float32)  8.27 us
  transfers between devices with their start and end apart: 6, of which 4 were waited for; matrix products, arithmetic and copies ran while one was open for 19% of the time, Pallas kernels for 0%

commit v1 on v0

--- a/solution.py
+++ b/solution.py
@@ -75,7 +75,15 @@
     chan_heads, gate_heads, step_heads, decay_heads = (
         lax.all_to_all(channels, "grp", split_axis=1, concat_axis=0, tiled=True),
         lax.all_to_all(gates, "grp", split_axis=1, concat_axis=0, tiled=True),
-        lax.all_to_all(step_size, "grp", split_axis=1, concat_axis=0, tiled=True),
+        jnp.concatenate(
+            lax.all_to_all(
+                jnp.stack(jnp.split(step_size, lax.axis_size("grp"), axis=1)),
+                axis_name="grp",
+                split_axis=0,
+                concat_axis=0,
+            ),
+            axis=0,
+        ),
         lax.all_to_all(log_decay, "grp", split_axis=1, concat_axis=0, tiled=True),
     )
     b_rows, c_rows = (

time: 235 us -> 235 us (level)
    unnamed x25 -> x23, local copies, waits for them, and re-layouts: 7.84 us -> 7.84 us
  transfers between devices with their start and end apart: 6 -> 6, of which waited for: 4 -> 4; matrix products, arithmetic and copies ran while one was open for 19% -> 20% of each run, Pallas kernels for 0% -> 0%
where the time goes in v1:
time: 235 us; the launch traced here: 234 us
  waiting for transfers between devices  54.3 us (23%)
  blocking collectives  51.9 us (22%)
  local copies, waits for them, and re-layouts  39 us (17%)
  matrix products  32.4 us (14%)
  other arithmetic  26.2 us (11%)
  starting transfers between devices  15.4 us (7%)
  between operations  14.3 us (6%)
    reduce_scatter x1, waiting for transfers between devices, local(): lax.psum_scatter(jnp.dot(normed, out_weight, preferred_element_type=jnp.f...  33.1 us
    unnamed x1, blocking collectives  22.7 us
    all_gather x1, blocking collectives, local(): lax.all_gather(c_proj, 'grp', axis=0, tiled=True)  17.5 us
    all_to_all x1, waiting for transfers between devices, local(): lax.all_to_all(channels, 'grp', split_axis=1, concat_axis=0, tiled=True)  15.1 us
    dot_general x1, matrix products, local_scan(): y_intra = jnp.einsum('qhij,qjhp->qihp', weights, inputs, precision=highest)  13.1 us
    convert_element_type x3, local copies, waits for them, and re-layouts, local_scan(): chan_f = chan_heads.astype(jnp.float32).reshape(piece_len, nheads, HD)  10.9 us
    select_n x7, other arithmetic, turn(): jnp.where(position < mine, new, old)  8.64 us
    convert_element_type x2, local copies, waits for them, and re-layouts, local(): gate_heads.astype(jnp.float32)  8.27 us
  transfers between devices with their start and end apart: 6, of which 4 were waited for; matrix products, arithmetic and copies ran while one was open for 20% of the time, Pallas kernels for 0%

profile of v1, /device:TPU:0, one launch (start us, length us, event | category | flops | bytes accessed | tf_op | source)
XLA Modules:
  0.0 233.9 jit_solution(3611515277049778883)
XLA Ops:
  6.5 1.3 all_to_all.36
  7.9 4.2 %all-to-all-start.2 = ((bf16[128,4,20]{0,2,1:T(8,128)(2,1)}), bf16[128,4,20]{0,2,1:T(8,128)(2,1)S(1)}, u32[]{:S(2)}, u32[]{:S(2)}) async-start(bf16[128,4,20]{0,2,1:T(8,128)(2,1)} %all_to_all.36), calls=%async_computation.2 | async-start | bytes 49152 | tf_op jit(solution)/shard_map/all_to_all | solution.py:87
  13.5 5.8 %all_gather.17 = bf16[512,128]{1,0:T(8,128)(2,1)S(1)} all-gather(bf16[128,128]{1,0:T(8,128)(2,1)} %param.15), channel_id=1, replica_groups=mesh['ctx'=8,'grp'=4] {'grp'}, dimensions={0}, use_global_device_ids=true | all-gather | bytes 163840 | tf_op jit(solution)/shard_map/all_gather | solution.py:90
  19.2 2.4 %copy.51 = bf16[128,5120]{0,1:T(8,128)(2,1)} copy(bf16[128,5120]{1,0:T(8,128)(2,1)} %param.13) | data formatting | bytes 2621440 | tf_op args[0]
  21.7 3.3 %all-to-all-start.1 = ((bf16[4,128,20]{1,2,0:T(8,128)(2,1)}), bf16[4,128,20]{1,2,0:T(8,128)(2,1)S(1)}, u32[]{:S(2)}, u32[]{:S(2)}) async-start(bf16[4,128,20]{1,2,0:T(8,128)(2,1)} %pad_maximum_fusion), calls=%async_computation.1 | async-start | bytes 49152 | tf_op jit(solution)/shard_map/all_to_all | solution.py:79
  25.1 1.2 reduce-window.6
  26.3 2.5 %all-to-all-done.1 = bf16[4,128,20]{1,2,0:T(8,128)(2,1)S(1)} async-done(((bf16[4,128,20]{1,2,0:T(8,128)(2,1)}), bf16[4,128,20]{1,2,0:T(8,128)(2,1)S(1)}, u32[]{:S(2)}, u32[]{:S(2)}) %all-to-all-start.1) | async-done | bytes 20512 | tf_op jit(solution)/shard_map/all_to_all | solution.py:79
  28.8 3.5 %all-to-all-start = ((bf16[128,4,1280]{0,2,1:T(8,128)(2,1)}), bf16[128,4,1280]{0,2,1:T(8,128)(2,1)S(1)}, u32[]{:S(2)}, u32[]{:S(2)}) async-start(bf16[128,4,1280]{0,2,1:T(8,128)(2,1)} %bitcast), calls=%async_computation | async-start | bytes 2621440 | tf_op jit(solution)/shard_map/all_to_all | solution.py:76
  34.5 15.1 %all-to-all-done = bf16[128,4,1280]{0,2,1:T(8,128)(2,1)S(1)} async-done(((bf16[128,4,1280]{0,2,1:T(8,128)(2,1)}), bf16[128,4,1280]{0,2,1:T(8,128)(2,1)S(1)}, u32[]{:S(2)}, u32[]{:S(2)}) %all-to-all-start) | async-done | bytes 1310752 | tf_op jit(solution)/shard_map/all_to_all | solution.py:76
  49.8 5.4 %copy.52 = f32[4,128,1280]{1,0,2:T(4,128)S(1)} copy(f32[4,128,1280]{1,2,0:T(8,128)S(1)} %convert_bitcast_fusion.1) | data formatting | bytes 5242880 | tf_op jit(solution)/shard_map/convert_element_type | solution.py:33
  55.2 3.3 %reshape.120 = f32[2,256,20,64]{1,0,3,2:T(2,128)} reshape(f32[4,128,1280]{1,0,2:T(4,128)S(1)} %copy.52) | data formatting | bytes 5242880 | tf_op jit(solution)/shard_map/convert_element_type | solution.py:33
  58.5 5.1 %broadcast_multiply_fusion = (f32[2,256,20,64]{1,0,3,2:T(2,128)S(1)}, f32[2,256,20,64]{1,0,3,2:T(2,128)}) fusion(f32[2,256,20]{1,0,2:T(2,128)S(1)} %get-tuple-element.189, f32[2,256,20,64]{1,0,3,2:T(2,128)} %reshape.120, f32[2,256,20]{1,0,2:T(2,128)S(1)} %reshape.121), kind=kLoop, calls=%fused_computation.39 | loop fusion | flops 1310720 | bytes 7946240 | tf_op jit(solution)/shard_map/mul | solution.py:50
  63.7 2.4 %fusion.22 = f32[2,20,64,128]{3,2,1,0:T(8,128)} fusion(bf16[2,256,128,1]{2,1,3,0:T(8,128)(2,1)S(1)} %bitcast.135, f32[2,256,20,64]{1,0,3,2:T(2,128)S(1)} %get-tuple-element.186), kind=kOutput, calls=%fused_computation.33 | convolution fusion | flops 1006632960 | bytes 4063232 | tf_op jit(solution)/shard_map/qjhp,qjn->qhpn/dot_general | solution.py:49
  66.0 4.3 %while.27 = (s32[]{:T(128)}, f32[20,64,128]{2,1,0:T(8,128)S(1)}, f32[2,20,64,128]{3,2,1,0:T(8,128)}, f32[2,20]{1,0:T(2,128)S(1)}, f32[2,20,64,128]{3,2,1,0:T(8,128)}, /*index=5*/s32[]{:T(128)}, s32[]{:T(128)}) while((s32[]{:T(128)}, f32[20,64,128]{2,1,0:T(8,128)S(1)}, f32[2,20,64,128]{3,2,1,0:T(8,128)}, f32[2,20]{1,0:T(2,128)S(1)}, ...), condition=%wide.region_3.4_spmd.clone, body=%wide.region_2.3_spmd.clone.sunk | while | flops 655363 | bytes 3277648 | solution.py:58
  66.0 0.9 bitcast_dynamic-update-slice_fusion.2
  67.0 1.2 bitcast_add_fusion.3
  68.2 0.9 bitcast_dynamic-update-slice_fusion.2
  69.1 1.2 bitcast_add_fusion.3
  70.4 0.8 copy-done
  71.2 2.5 %copy.68 = bf16[128,5120]{0,1:T(8,128)(2,1)} copy(bf16[128,5120]{1,0:T(8,128)(2,1)} %param.14) | data formatting | bytes 2621440 | tf_op args[1]
  73.7 4.3 %all-to-all-start.3 = ((bf16[128,4,1280]{0,2,1:T(8,128)(2,1)}), bf16[128,4,1280]{0,2,1:T(8,128)(2,1)}, u32[]{:S(2)}, u32[]{:S(2)}) async-start(bf16[128,4,1280]{0,2,1:T(8,128)(2,1)} %bitcast.131), calls=%async_computation.3 | async-start | bytes 2621440 | tf_op jit(solution)/shard_map/all_to_all | solution.py:77
  79.3 17.5 %all_gather.16 = bf16[512,128]{1,0:T(8,128)(2,1)S(1)} all-gather(bf16[128,128]{1,0:T(8,128)(2,1)} %param.16), channel_id=1, replica_groups=mesh['ctx'=8,'grp'=4] {'grp'}, dimensions={0}, use_global_device_ids=true | all-gather | bytes 163840 | tf_op jit(solution)/shard_map/all_gather | solution.py:91
  97.4 1.0 fusion.28
  98.5 1.4 copy.57
  100.7 22.7 %all-reduce = f32[160]{0:T(256)S(1)} all-reduce(f32[160]{0:T(256)S(1)} %exponential_dynamic-update-slice_fusion), channel_id=2, replica_groups=mesh['ctx'=8,'grp'=4] {'ctx'}, use_global_device_ids=true, to_apply=%add | all-reduce | flops 160 | bytes 1280
  125.0 2.1 reshape.123
  127.1 13.1 %fusion.2 = f32[2,20,64,256]{3,2,1,0:T(8,128)S(1)} fusion(f32[2,256,256]{2,1,0:T(8,128)} %fusion.28, f32[2,20,256]{2,1,0:T(8,128)} %copy.57, pred[256,256]{1,0:T(8,128)(4,1)S(1)} %copy-done.3, f32[2,256,20,64]{1,0,3,2:T(2,128)} %get-tuple-element.187), kind=kOutput, calls=%fused_computation.7 | convolution fusion | flops 2021130240 | bytes 5873664 | tf_op jit(solution)/shard_map/qhij,qjhp->qihp/dot_general | solution.py:45
  140.2 1.3 fusion.21
  141.6 1.9 copy.74
  143.5 1.6 copy.69
  145.1 1.7 convert_bitcast_fusion
  146.8 4.1 %copy.71 = f32[4,128,1280]{1,0,2:T(4,128)} copy(f32[4,128,1280]{2,1,0:T(8,128)} %convert_bitcast_fusion) | data formatting | bytes 5242880 | tf_op jit(solution)/shard_map/convert_element_type | solution.py:112
  151.0 4.1 %reshape.125 = f32[512,20,64]{0,2,1:T(8,128)} reshape(f32[4,128,1280]{1,0,2:T(4,128)} %copy.71) | data formatting | bytes 5242880 | tf_op jit(solution)/shard_map/convert_element_type | solution.py:112
  155.1 3.5 %all-gather.4.cloned.1.call-done = f32[160,64,128]{2,1,0:T(8,128)} async-done(((f32[20,64,128]{2,1,0:T(8,128)}), f32[160,64,128]{2,1,0:T(8,128)}) %all-gather.4.cloned.1.call-update) | async-done | bytes 5242896 | tf_op jit(solution)/shard_map/all_gather | solution.py:14
  158.6 8.9 %while.28 = (s32[]{:T(128)}, f32[20,64,128]{2,1,0:T(8,128)S(1)}, s32[]{:T(128)}, f32[8,20]{1,0:T(8,128)S(1)}, f32[8,20,64,128]{3,2,1,0:T(8,128)}, /*index=5*/s32[]{:T(128)}, s32[]{:T(128)}) while((s32[]{:T(128)}, f32[20,64,128]{2,1,0:T(8,128)S(1)}, s32[]{:T(128)}, f32[8,20]{1,0:T(8,128)S(1)}, f32[8,20,64,128]{3,2,1,0:T(8,128)}, ...), condition=%wide.region_6.7_spmd.clone, body=%wide.region_5.6_spmd.clone.sunk | while | flops 655364 | bytes 1966425 | solution.py:23
  158.7 1.2 fusion.40
  159.9 1.2 fusion.40
  161.2 1.2 fusion.40
  162.5 1.2 fusion.40
  163.8 1.2 fusion.40
  165.0 1.2 fusion.40
  166.3 1.2 fusion.40
  167.6 6.9 %multiply_reduce_fusion = (f32[512]{0:T(512)S(1)}, f32[512,20,64]{0,2,1:T(8,128)}) fusion(f32[512,20,64]{0,2,1:T(8,128)} %reshape.125, f32[512,20,64]{0,2,1:T(8,128)} %reshape.123, f32[20]{0:T(128)S(1)} %copy-done.6, f32[512,20,64]{0,2,1:T(8,128)} %bitcast.132, f32[512,20]{0,1:T(8,128)S(1)} %bitcast.143, f32[20,64,128]{2,1,0:T(8,128)S(1)} %get-tuple-element.129, ...), kind=kOutput, calls=%fused_computation.37 | convolution fusion | flops 1013841408 | bytes 11315280 | tf_op jit(solution)/shard_map/tn,hpn->thp/dot_general | solution.py:107
  174.4 3.2 %copy.70 = f32[512,1280]{1,0:T(8,128)} copy(f32[512,1280]{0,1:T(8,128)} %bitcast.133) | data formatting | bytes 5242880 | tf_op jit(solution)/shard_map/reshape | solution.py:111
  177.7 5.9 %psum.7 = f32[512]{0:T(512)S(1)} all-reduce(f32[512]{0:T(512)S(1)} %get-tuple-element.197), channel_id=1, replica_groups=mesh['ctx'=8,'grp'=4] {'grp'}, use_global_device_ids=true, to_apply=%region_9.10 | all-reduce | flops 512 | bytes 4096 | tf_op jit(solution)/shard_map/psum | solution.py:114
  183.6 2.6 %fusion.25 = bf16[512,1280]{1,0:T(8,128)(2,1)S(1)} fusion(f32[512,1280]{1,0:T(8,128)} %copy.70, bf16[128,4,1280]{2,0,1:T(8,128)(2,1)S(1)} %copy.69, f32[1280]{0:T(1024)S(1)} %copy-done.5, f32[512]{0:T(512)S(1)} %add_rsqrt_fusion), kind=kLoop, calls=%fused_computation.38 | loop fusion | flops 5898240 | bytes 5250048 | tf_op jit(solution)/shard_map/convert_element_type | solution.py:116
  186.2 7.7 %convolution_convert_fusion = bf16[512,2560]{1,0:T(8,128)(2,1)} fusion(bf16[512,1280]{1,0:T(8,128)(2,1)S(1)} %fusion.25, bf16[1280,2560]{1,0:T(8,128)(2,1)} %param.21), kind=kOutput, calls=%fused_computation.17 | convolution fusion | flops 3356753920 | bytes 10485760 | tf_op jit(solution)/shard_map/dot_general | solution.py:118
  193.9 33.1 %reduce-scatter.2.cloned.1.call-done = bf16[128,2560]{1,0:T(8,128)(2,1)} async-done(((bf16[512,2560]{1,0:T(8,128)(2,1)}), bf16[128,2560]{1,0:T(8,128)(2,1)}) %reduce-scatter.2.cloned.1.call-update) | async-done | bytes 655376 | tf_op jit(solution)/shard_map/reduce_scatter | solution.py:117
  (67 shorter events, 7.5 us)
Async XLA Ops:
  7.9 13.8 %all-to-all-start.2 = ((bf16[128,4,20]{0,2,1:T(8,128)(2,1)}), bf16[128,4,20]{0,2,1:T(8,128)(2,1)S(1)}, u32[]{:S(2)}, u32[]{:S(2)}) async-start(bf16[128,4,20]{0,2,1:T(8,128)(2,1)} %all_to_all.36), calls=%async_computation.2 | async-start | bytes 49152 | tf_op jit(solution)/shard_map/all_to_all | solution.py:87
  21.7 7.1 %all-to-all-start.1 = ((bf16[4,128,20]{1,2,0:T(8,128)(2,1)}), bf16[4,128,20]{1,2,0:T(8,128)(2,1)S(1)}, u32[]{:S(2)}, u32[]{:S(2)}) async-start(bf16[4,128,20]{1,2,0:T(8,128)(2,1)} %pad_maximum_fusion), calls=%async_computation.1 | async-start | bytes 49152 | tf_op jit(solution)/shard_map/all_to_all | solution.py:79
  28.8 20.8 %all-to-all-start = ((bf16[128,4,1280]{0,2,1:T(8,128)(2,1)}), bf16[128,4,1280]{0,2,1:T(8,128)(2,1)S(1)}, u32[]{:S(2)}, u32[]{:S(2)}) async-start(bf16[128,4,1280]{0,2,1:T(8,128)(2,1)} %bitcast), calls=%async_computation | async-start | bytes 2621440 | tf_op jit(solution)/shard_map/all_to_all | solution.py:76
  32.4 126.3 %all-gather.4.cloned.1.call-start = ((), (), s32[]{:S(2)}) async-start(), calls=%async_computation.6 | async-start | bytes 5898240 | tf_op jit(solution)/shard_map/all_gather | solution.py:14
  32.8 16.8 %copy-start.2 = (f32[2,20,256]{2,0,1:T(2,128)}, f32[2,20,256]{2,0,1:T(2,128)S(1)}, u32[]{:S(2)}) copy-start(f32[2,20,256]{2,0,1:T(2,128)S(1)} %reduce_window_sum.35) | copy-start | bytes 122884
  70.4 0.8 copy-start
  71.2 6.9 %copy-start.7 = (u32[32]{0:T(128)S(1)}, u32[32]{0:T(128)}, u32[]{:S(2)}) copy-start(u32[32]{0:T(128)} %constant.61) | copy-start | bytes 388
  73.7 69.8 %all-to-all-start.3 = ((bf16[128,4,1280]{0,2,1:T(8,128)(2,1)}), bf16[128,4,1280]{0,2,1:T(8,128)(2,1)}, u32[]{:S(2)}, u32[]{:S(2)}) async-start(bf16[128,4,1280]{0,2,1:T(8,128)(2,1)} %bitcast.131), calls=%async_computation.3 | async-start | bytes 2621440 | tf_op jit(solution)/shard_map/all_to_all | solution.py:77
  78.0 149.0 %reduce-scatter.2.cloned.1.call-start = ((), (), s32[]{:S(2)}) async-start(), calls=%async_computation.5 | async-start | bytes 3276800 | tf_op jit(solution)/shard_map/reduce_scatter | solution.py:117
  125.0 2.1 copy-start.3
  127.1 13.1 %copy-start.1 = (f32[2,20,64,128]{3,2,1,0:T(8,128)S(1)}, f32[2,20,64,128]{3,2,1,0:T(8,128)}, u32[]{:S(2)}) copy-start(f32[2,20,64,128]{3,2,1,0:T(8,128)} %get-tuple-element.127) | copy-start | bytes 3932164
  158.6 8.9 %copy-start.4 = (f32[3,8,2,256]{3,1,2,0:T(8,128)S(1)}, f32[3,8,2,256]{3,1,2,0:T(8,128)}, u32[]{:S(2)}) copy-start(f32[3,8,2,256]{3,1,2,0:T(8,128)} %copy.75) | copy-start | bytes 147460
  158.6 8.9 %copy-start.6 = (f32[20]{0:T(128)S(1)}, f32[20]{0:T(128)}, u32[]{:S(2)}) copy-start(f32[20]{0:T(128)} %param.19) | copy-start | bytes 244
  174.4 9.2 %copy-start.5 = (f32[1280]{0:T(1024)S(1)}, f32[1280]{0:T(1024)}, u32[]{:S(2)}) copy-start(f32[1280]{0:T(1024)} %param.20) | copy-start | bytes 15364
Sparse Core Ops, SparseCore 0:
  71.3 87.2 all-gather.3
  194.1 32.9 reduce-scatter.1
